TPU v7x, 32 devices: a whole 2x2x4 slice. The times are simulated.
32 devices in a mesh: occ: 16 (over z, y, core), vir: 2 (over x).
Axes of the slice: x: 2, y: 2, z: 4, core: 2. Of those that a mesh axis runs over, the one named last changes fastest.
Arguments:
- lambda_triples: bfloat16 [256, 320, 320], P('occ', 'vir'), may hold values from -6 to 6
- amplitude_triples: bfloat16 [256, 320, 320], P('occ', 'vir'), may hold values from -6 to 6
- spin_extent: int32 [256], P('occ'), may hold values from 80 to 320
- ladder_weight: bfloat16 [320, 320], P(None, 'vir'), may hold values from -0.3125 to 0.3125
- cycle_weight: bfloat16 [320, 40], replicated, may hold values from -0.3125 to 0.3125
- lambda_doubles: bfloat16 [40, 320], P(None, 'vir'), may hold values from -1 to 1
Outputs:
- residual: bfloat16 [256, 320, 320], P('occ', 'vir')
All inputs are finite; a program needn't handle non-finite values.
Results may differ from a plain program's by a relative error of at most 0.0043.
Values may be sent and summed in bfloat16 or wider, within the bound.
No kernel may reach another device: no remote copies, remote signals or barrier semaphores. Data moves between devices by JAX's collectives and lax.ppermute only.
A program may use at most 64 MiB of HBM per device.

v0:
```python
import jax
import jax.numpy as jnp
from jax import lax
from jax.sharding import PartitionSpec as P


def on_device(
    lambda_triples, amplitude_triples, spin_extent, ladder_weight, cycle_weight, lambda_doubles
):
    f32 = jnp.float32
    width = lambda_triples.shape[2]
    triples_all = lambda_triples.shape[0] * lax.axis_size("occ")
    columns = jnp.arange(width, dtype=jnp.int32)
    keep = columns[None, :] < spin_extent[:, None]
    masked = jnp.where(keep[:, None, :], lambda_triples, jnp.zeros_like(lambda_triples))
    ladder_full, doubles_full = (
        lax.all_gather(ladder_weight, "vir", axis=1, tiled=True),
        lax.all_gather(lambda_doubles, "vir", axis=1, tiled=True),
    )
    ladder_term = jnp.einsum("tae,eb->tab", masked, ladder_full, preferred_element_type=f32)
    cycle_mid = jnp.einsum(
        "tae,em->tam", amplitude_triples, cycle_weight, preferred_element_type=f32
    ).astype(jnp.bfloat16)
    cycle_term = jnp.einsum("tam,mb->tab", cycle_mid, doubles_full, preferred_element_type=f32)
    partial_density = jnp.einsum(
        "tae,tbe->ab",
        masked,
        lax.all_gather(amplitude_triples, "vir", axis=1, tiled=True),
        preferred_element_type=f32,
    )
    density = lax.psum(partial_density, "occ")
    density = (density / jnp.sqrt(f32(triples_all * width))).astype(jnp.bfloat16)
    density_term = jnp.einsum(
        "ac,tcb->tab",
        density,
        lax.all_gather(masked, "vir", axis=1, tiled=True),
        preferred_element_type=f32,
    )
    density_term = density_term / jnp.sqrt(f32(width))
    return (ladder_term + cycle_term + density_term).astype(jnp.bfloat16)


def solution(mesh):
    return jax.shard_map(
        on_device,
        mesh=mesh,
        in_specs=(
            P("occ", "vir", None),
            P("occ", "vir", None),
            P("occ"),
            P(None, "vir"),
            P(),
            P(None, "vir"),
        ),
        out_specs=P("occ", "vir", None),
        check_vma=False,
    )
```

profile of v0, /device:TPU:8, one launch (start us, length us, event | category | flops | bytes accessed | tf_op | source)
XLA Modules:
  0.0 227.4 jit_solution(11360172198900712387)
XLA Ops:
  6.5 0.0 copy-start
  6.5 0.0 copy-start.3
  6.5 0.0 copy-start.2
  6.5 0.0 all-gather.6.cloned.1.call-start
  6.5 0.7 all-gather.6.cloned.1.call-update
  7.3 0.0 all-gather.4.cloned.1.call-start
  7.3 0.7 iota_compare_fusion
  8.0 3.0 %broadcast_select_fusion = bf16[16,160,320]{2,1,0:T(8,128)(2,1)} fusion(bf16[16,160,320]{2,1,0:T(8,128)(2,1)} %param.6, pred[16,320]{1,0:T(8,128)(4,1)S(1)} %iota_compare_fusion), kind=kLoop, calls=%fused_computation.2 | loop fusion | flops 819200 | bytes 3281920 | tf_op jit(solution)/shard_map/jit(_where)/select_n | solution.py:15
  11.1 0.0 copy-start.1
  11.1 0.0 all-gather.4.cloned.1.call-update
  11.1 0.0 all-reduce.2.cloned.1.call-start
  11.2 0.0 copy-done.3
  11.2 4.6 %all-gather = bf16[2,160,40]{1,2,0:T(8,128)(2,1)S(1)} all-gather(bf16[1,160,40]{1,2,0:T(8,128)(2,1)S(1)} %bitcast.27), channel_id=1, replica_groups=mesh['occ'=16,'vir'=2] {'vir'}, dimensions={0}, use_global_device_ids=true | all-gather | bytes 38400 | tf_op jit(solution)/shard_map/all_gather | solution.py:18
  15.8 0.1 reshape.21
  15.9 0.0 copy-done.2
  15.9 6.4 %all_gather.12 = bf16[320,320]{0,1:T(8,128)(2,1)S(1)} all-gather(bf16[320,160]{0,1:T(8,128)(2,1)S(1)} %copy-done.2), channel_id=1, replica_groups=mesh['occ'=16,'vir'=2] {'vir'}, dimensions={1}, use_global_device_ids=true | all-gather | bytes 307200 | tf_op jit(solution)/shard_map/all_gather | solution.py:17
  22.3 4.9 %fusion.2 = f32[16,160,320]{2,1,0:T(8,128)} fusion(bf16[16,160,320]{2,1,0:T(8,128)(2,1)} %broadcast_select_fusion, bf16[320,320]{0,1:T(8,128)(2,1)S(1)} %all_gather.12), kind=kOutput, calls=%fused_computation.6 | convolution fusion | flops 524288000 | bytes 5120000 | tf_op jit(solution)/shard_map/tae,eb->tab/dot_general | solution.py:20
  27.2 36.7 %all-gather.6.cloned.1.call-done = bf16[16,320,320]{2,1,0:T(8,128)(2,1)} async-done(((bf16[16,160,320]{2,1,0:T(8,128)(2,1)}), bf16[16,320,320]{2,1,0:T(8,128)(2,1)}) %all-gather.6.cloned.1.call-update) | async-done | bytes 3276816 | tf_op jit(solution)/shard_map/all_gather | solution.py:28
  63.9 0.0 copy-done.1
  63.9 4.4 %convolution_bitcast_fusion = f32[160,320]{1,0:T(8,128)} fusion(bf16[16,160,320]{2,1,0:T(8,128)(2,1)S(1)} %copy-done.1, bf16[16,320,320]{2,1,0:T(8,128)(2,1)} %all-gather.6.cloned.1.call-done), kind=kOutput, calls=%fused_computation.5 | convolution fusion | flops 524288000 | bytes 5120000 | tf_op jit(solution)/shard_map/tae,tbe->ab/dot_general | solution.py:25
  68.3 0.0 all-reduce.2.cloned.1.call-update
  68.3 0.0 copy-done
  68.3 5.2 %fusion.1 = f32[16,160,320]{2,1,0:T(8,128)} fusion(bf16[320,40,1]{0,1,2:T(8,128)(2,1)S(1)} %reshape.21, bf16[16,160,320]{2,1,0:T(8,128)(2,1)} %param.7, bf16[320,40]{0,1:T(8,128)(2,1)S(1)} %copy-done), kind=kOutput, calls=%fused_computation.4 | convolution fusion | flops 131174400 | bytes 4966400 | tf_op jit(solution)/shard_map/tam,mb->tab/dot_general | solution.py:24
  73.5 46.9 %all-gather.4.cloned.1.call-done = bf16[16,320,320]{2,1,0:T(8,128)(2,1)} async-done(((bf16[16,160,320]{2,1,0:T(8,128)(2,1)}), bf16[16,320,320]{2,1,0:T(8,128)(2,1)}) %all-gather.4.cloned.1.call-update) | async-done | bytes 3276816 | tf_op jit(solution)/shard_map/all_gather | solution.py:36
  120.4 93.5 %all-reduce.2.cloned.1.call-done = f32[160,320]{1,0:T(8,128)} async-done(((f32[160,320]{1,0:T(8,128)}), f32[160,320]{1,0:T(8,128)}) %all-reduce.2.cloned.1.call-update) | async-done | bytes 204816 | tf_op jit(solution)/shard_map/psum | solution.py:31
  213.9 7.0 %fusion = bf16[16,160,320]{2,1,0:T(8,128)(2,1)} fusion(f32[16,160,320]{2,1,0:T(8,128)} %fusion.2, f32[16,160,320]{2,1,0:T(8,128)} %fusion.1, bf16[16,320,320]{2,1,0:T(8,128)(2,1)} %all-gather.4.cloned.1.call-done, f32[160,320]{1,0:T(8,128)} %all-reduce.2.cloned.1.call-done), kind=kOutput, calls=%fused_computation.1 | convolution fusion | flops 527667200 | bytes 11673600 | tf_op jit(solution)/shard_map/ac,tcb->tab/dot_general | solution.py:33
  (1 shorter events, 0.0 us)
Async XLA Ops:
  6.5 61.8 %copy-start = (bf16[320,40]{0,1:T(8,128)(2,1)S(1)}, bf16[320,40]{0,1:T(8,128)(2,1)}, u32[]{:S(2)}) copy-start(bf16[320,40]{0,1:T(8,128)(2,1)} %param.10) | copy-start | bytes 76804
  6.5 4.6 %copy-start.3 = (bf16[40,160]{1,0:T(8,128)(2,1)S(1)}, bf16[40,160]{1,0:T(8,128)(2,1)}, u32[]{:S(2)}) copy-start(bf16[40,160]{1,0:T(8,128)(2,1)} %param.11) | copy-start | bytes 38404
  6.5 9.4 %copy-start.2 = (bf16[320,160]{0,1:T(8,128)(2,1)S(1)}, bf16[320,160]{0,1:T(8,128)(2,1)}, u32[]{:S(2)}) copy-start(bf16[320,160]{0,1:T(8,128)(2,1)} %param.9) | copy-start | bytes 307204
  6.5 57.4 %all-gather.6.cloned.1.call-start = ((), (), s32[]{:S(2)}) async-start(), calls=%async_computation.1 | async-start | bytes 5898240 | tf_op jit(solution)/shard_map/all_gather | solution.py:28
  7.3 113.1 %all-gather.4.cloned.1.call-start = ((), (), s32[]{:S(2)}) async-start(), calls=%async_computation | async-start | bytes 5898240 | tf_op jit(solution)/shard_map/all_gather | solution.py:36
  11.1 52.8 %copy-start.1 = (bf16[16,160,320]{2,1,0:T(8,128)(2,1)S(1)}, bf16[16,160,320]{2,1,0:T(8,128)(2,1)}, u32[]{:S(2)}) copy-start(bf16[16,160,320]{2,1,0:T(8,128)(2,1)} %broadcast_select_fusion) | copy-start | bytes 4915204
  11.1 202.8 %all-reduce.2.cloned.1.call-start = ((), (), s32[]{:S(2)}) async-start(), calls=%async_computation.2 | async-start | bytes 491520 | tf_op jit(solution)/shard_map/psum | solution.py:31
Sparse Core Ops, SparseCore 0:
  8.9 54.9 all-gather.5
  65.4 54.8 all-gather.3
  123.8 90.0 all-reduce.1
where the time goes:
time: 228 us; the launch traced here: 227 us
  waiting for transfers between devices  178 us (78%)
  matrix products  21.4 us (9%)
  between operations  13.1 us (6%)
  blocking collectives  11 us (5%)
  other arithmetic  3.77 us (2%)
    psum x1, waiting for transfers between devices, on_device(): density = lax.psum(partial_density, 'occ')  93.5 us
    all_gather x1, waiting for transfers between devices, on_device(): lax.all_gather(masked, 'vir', axis=1, tiled=True)  46.9 us
    all_gather x1, waiting for transfers between devices, on_device(): lax.all_gather(amplitude_triples, 'vir', axis=1, tiled=True)  36.7 us
    dot_general x1, matrix products, on_device(): jnp.einsum('ac,tcb->tab', density, lax.all_gather(masked, 'vir', axis=1,...  6.97 us
    all_gather x1, blocking collectives, on_device(): lax.all_gather(ladder_weight, 'vir', axis=1, tiled=True)  6.43 us
    dot_general x1, matrix products, on_device(): jnp.einsum('tam,mb->tab', cycle_mid, doubles_full, preferred_element_type...  5.16 us
    dot_general x1, matrix products, on_device(): jnp.einsum('tae,eb->tab', masked, ladder_full, preferred_element_type=f32)  4.91 us
    all_gather x1, blocking collectives, on_device(): lax.all_gather(lambda_doubles, 'vir', axis=1, tiled=True)  4.59 us
  transfers between devices with their start and end apart: 3, of which 3 were waited for; matrix products, arithmetic and copies ran while one was open for 8% of the time, Pallas kernels for 0%

commit v1 on v0

--- a/solution.py
+++ b/solution.py
@@ -30,12 +30,32 @@
     )
     density = lax.psum(partial_density, "occ")
     density = (density / jnp.sqrt(f32(triples_all * width))).astype(jnp.bfloat16)
+    block_out, extra = (lax.axis_size("vir"), lax.axis_index("vir"))
+    gallery = []
+    k0 = 0
+    while k0 < block_out:
+        gallery.append((k0, (k0 - 1) % block_out))
+        k0 += 1
+    everything = masked.shape[1]
+    work_now = masked
     density_term = jnp.einsum(
         "ac,tcb->tab",
-        density,
-        lax.all_gather(masked, "vir", axis=1, tiled=True),
+        lax.dynamic_slice_in_dim(density, extra * everything, work_now.shape[1], axis=1),
+        work_now,
         preferred_element_type=f32,
     )
+    k = 1
+    while k < block_out:
+        work_now = lax.ppermute(work_now, "vir", gallery)
+        density_term = density_term + jnp.einsum(
+            "ac,tcb->tab",
+            lax.dynamic_slice_in_dim(
+                density, (extra + k) % block_out * everything, work_now.shape[1], axis=1
+            ),
+            work_now,
+            preferred_element_type=f32,
+        )
+        k += 1
     density_term = density_term / jnp.sqrt(f32(width))
     return (ladder_term + cycle_term + density_term).astype(jnp.bfloat16)
 

time: 228 us -> 212 us (0.930)
  waiting for transfers between devices: 178 us -> 87.9 us
  blocking collectives: 11 us -> 85.8 us
  matrix products: 21.4 us -> 18.8 us
    all_gather x1, blocking collectives: 4.59 us -> 77.3 us  [on_device(): lax.all_gather(lambda_doubles, 'vir', axis=1, tiled=True)]
    all_gather x1 -> x0, waiting for transfers between devices: 46.9 us -> none  [on_device(): lax.all_gather(masked, 'vir', axis=1, tiled=True)]
    all_gather x1, waiting for transfers between devices: 36.7 us -> 0.01 us  [on_device(): lax.all_gather(amplitude_triples, 'vir', axis=1, tiled=True)]
    psum x1, waiting for transfers between devices: 93.5 us -> 87.2 us  [on_device(): density = lax.psum(partial_density, 'occ')]
    dot_general x1 -> x2, matrix products: 6.97 us -> 6.12 us  [the longest x1 5.39 us: on_device(): jnp.einsum('ac,tcb->tab', lax.dynamic_slice_in_dim(density, (extra + k) %...]
  transfers between devices with their start and end apart: 3 -> 3, of which waited for: 3 -> 1; matrix products, arithmetic and copies ran while one was open for 8% -> 8% of each run, Pallas kernels for 0% -> 0%
where the time goes in v1:
time: 212 us
  waiting for transfers between devices  87.9 us (41%)
  blocking collectives  85.8 us (40%)
  matrix products  18.8 us (9%)
  between operations  13.5 us (6%)
  other arithmetic  2.85 us (1%)
    psum x1, waiting for transfers between devices, on_device(): density = lax.psum(partial_density, 'occ')  87.2 us
    all_gather x1, blocking collectives, on_device(): lax.all_gather(lambda_doubles, 'vir', axis=1, tiled=True)  77.3 us
    all_gather x1, blocking collectives, on_device(): lax.all_gather(ladder_weight, 'vir', axis=1, tiled=True)  8.54 us
    dot_general x1, matrix products, on_device(): jnp.einsum('ac,tcb->tab', lax.dynamic_slice_in_dim(density, (extra + k) %...  5.39 us
    dot_general x1, matrix products, on_device(): jnp.einsum('tam,mb->tab', cycle_mid, doubles_full, preferred_element_type...  5.07 us
    dot_general x1, matrix products, on_device(): jnp.einsum('tae,tbe->ab', masked, lax.all_gather(amplitude_triples, 'vir'...  4.42 us
  transfers between devices with their start and end apart: 3, of which 1 were waited for; matrix products, arithmetic and copies ran while one was open for 8% of the time, Pallas kernels for 0%

profile of v1, /device:TPU:8, one launch (start us, length us, event | category | flops | bytes accessed | tf_op | source)
XLA Modules:
  0.0 212.0 jit_solution(5111556831285195092)
XLA Ops:
  6.5 0.0 copy-start
  6.5 0.0 copy-start.4
  6.5 0.0 all-gather.3.cloned.1.call-start
  6.5 0.7 all-gather.3.cloned.1.call-update
  7.3 0.0 all-reduce.2.cloned.1.call-start
  7.3 0.0 copy-done.4
  7.3 0.1 iota_compare_fusion
  7.4 0.0 copy-start.3
  7.4 0.0 copy-start.2
  7.4 1.8 broadcast_select_fusion
  9.2 1.6 collective-permute-start
  10.8 0.0 copy-done.3
  10.8 77.3 %all-gather = bf16[2,160,40]{1,2,0:T(8,128)(2,1)S(1)} all-gather(bf16[1,160,40]{1,2,0:T(8,128)(2,1)S(1)} %bitcast.31), channel_id=1, replica_groups=mesh['occ'=16,'vir'=2] {'vir'}, dimensions={0}, use_global_device_ids=true | all-gather | bytes 38400 | tf_op jit(solution)/shard_map/all_gather | solution.py:18
  88.1 0.1 reshape.21
  88.2 0.0 copy-done.2
  88.2 8.5 %all_gather.9 = bf16[320,320]{0,1:T(8,128)(2,1)S(1)} all-gather(bf16[320,160]{0,1:T(8,128)(2,1)S(1)} %copy-done.2), channel_id=1, replica_groups=mesh['occ'=16,'vir'=2] {'vir'}, dimensions={1}, use_global_device_ids=true | all-gather | bytes 307200 | tf_op jit(solution)/shard_map/all_gather | solution.py:17
  96.8 3.2 %fusion.2 = f32[16,160,320]{2,1,0:T(8,128)} fusion(bf16[16,160,320]{2,1,0:T(8,128)(2,1)S(1)} %broadcast_select_fusion, bf16[320,320]{0,1:T(8,128)(2,1)S(1)} %all_gather.9), kind=kOutput, calls=%fused_computation.6 | convolution fusion | flops 524288000 | bytes 5120000 | tf_op jit(solution)/shard_map/tae,eb->tab/dot_general | solution.py:20
  100.0 0.0 all-gather.3.cloned.1.call-done
  100.0 4.4 %convolution_bitcast_fusion = f32[160,320]{1,0:T(8,128)} fusion(bf16[16,160,320]{2,1,0:T(8,128)(2,1)S(1)} %broadcast_select_fusion, bf16[16,320,320]{2,1,0:T(8,128)(2,1)} %all-gather.3.cloned.1.call-done), kind=kOutput, calls=%fused_computation.5 | convolution fusion | flops 524288000 | bytes 5120000 | tf_op jit(solution)/shard_map/tae,tbe->ab/dot_general | solution.py:25
  104.4 0.0 all-reduce.2.cloned.1.call-update
  104.4 0.0 copy-done
  104.4 5.1 %fusion.1 = f32[16,160,320]{2,1,0:T(8,128)} fusion(bf16[320,40,1]{0,1,2:T(8,128)(2,1)S(1)} %reshape.21, bf16[16,160,320]{2,1,0:T(8,128)(2,1)} %param.7, bf16[320,40]{0,1:T(8,128)(2,1)S(1)} %copy-done), kind=kOutput, calls=%fused_computation.4 | convolution fusion | flops 131174400 | bytes 4966400 | tf_op jit(solution)/shard_map/tam,mb->tab/dot_general | solution.py:24
  109.5 87.2 %all-reduce.2.cloned.1.call-done = f32[160,320]{1,0:T(8,128)} async-done(((f32[160,320]{1,0:T(8,128)}), f32[160,320]{1,0:T(8,128)}) %all-reduce.2.cloned.1.call-update) | async-done | bytes 204816 | tf_op jit(solution)/shard_map/psum | solution.py:31
  196.7 1.0 multiply_convert_fusion
  197.6 0.0 copy-start.1
  197.6 0.7 fusion.5
  198.4 0.0 collective-permute-done
  198.4 1.4 copy-done.1
  199.7 5.4 %fusion = bf16[16,160,320]{2,1,0:T(8,128)(2,1)} fusion(f32[16,320,160]{1,2,0:T(8,128)S(1)} %fusion.5, f32[16,160,320]{2,1,0:T(8,128)} %fusion.2, f32[16,160,320]{2,1,0:T(8,128)S(1)} %copy-done.1, bf16[16,160,320]{2,1,0:T(8,128)(2,1)} %collective-permute-done, bf16[160,320]{1,0:T(8,128)(2,1)S(1)} %multiply_convert_fusion, s32[]{:T(128)S(6)} %select_n.20), kind=kOutput, calls=%fused_computation.1 | convolution fusion | flops 266240000 | bytes 14499844 | tf_op jit(solution)/shard_map/ac,tcb->tab/dot_general | solution.py:50
  (1 shorter events, 0.0 us)
Async XLA Ops:
  6.5 97.9 %copy-start = (bf16[320,40]{0,1:T(8,128)(2,1)S(1)}, bf16[320,40]{0,1:T(8,128)(2,1)}, u32[]{:S(2)}) copy-start(bf16[320,40]{0,1:T(8,128)(2,1)} %param.10) | copy-start | bytes 76804
  6.5 0.8 copy-start.4
  6.5 93.4 %all-gather.3.cloned.1.call-start = ((), (), s32[]{:S(2)}) async-start(), calls=%async_computation | async-start | bytes 5898240 | tf_op jit(solution)/shard_map/all_gather | solution.py:28
  7.3 189.4 %all-reduce.2.cloned.1.call-start = ((), (), s32[]{:S(2)}) async-start(), calls=%async_computation.1 | async-start | bytes 491520 | tf_op jit(solution)/shard_map/psum | solution.py:31
  7.4 3.4 %copy-start.3 = (bf16[40,160]{1,0:T(8,128)(2,1)S(1)}, bf16[40,160]{1,0:T(8,128)(2,1)}, u32[]{:S(2)}) copy-start(bf16[40,160]{1,0:T(8,128)(2,1)} %param.11) | copy-start | bytes 38404
  7.4 80.8 %copy-start.2 = (bf16[320,160]{0,1:T(8,128)(2,1)S(1)}, bf16[320,160]{0,1:T(8,128)(2,1)}, u32[]{:S(2)}) copy-start(bf16[320,160]{0,1:T(8,128)(2,1)} %param.9) | copy-start | bytes 307204
  9.2 189.1 %collective-permute-start = (bf16[16,160,320]{2,1,0:T(8,128)(2,1)S(1)}, bf16[16,160,320]{2,1,0:T(8,128)(2,1)}, u32[]{:S(2)}, u32[]{:S(2)}) collective-permute-start(bf16[16,160,320]{2,1,0:T(8,128)(2,1)S(1)} %broadcast_select_fusion), channel_id=1, source_target_pairs={{0,1},{1,0},{2,3},{3,2},{4,5},{5,4},{6,7},{7,6},{8,9},{9,8},{10,11... | collective-permute-start | bytes 4915208 | tf_op jit(solution)/shard_map/ppermute | solution.py:49
  197.6 2.1 copy-start.1
Sparse Core Ops, SparseCore 0:
  8.9 90.3 all-gather.2
  104.5 92.0 all-reduce.1
